TPU v7x, 128 devices: a whole 4x4x4 slice. The times are simulated.
128 devices in a mesh: row: 8 (over x, y_hi), col: 16 (over y_lo, z, core).
Axes of the slice: x: 4, y: 4 (y_hi: 2, y_lo: 2; y = y_hi * 2 + y_lo), z: 4, core: 2. Of those that a mesh axis runs over, the one named last changes fastest.
Arguments:
- train_inputs: bfloat16 [512, 8192], P(('row', 'col')), may hold values from -6 to 6
- train_grads: bfloat16 [512, 8192], P(('row', 'col')), may hold values from -6 to 6
- query_inputs: bfloat16 [256, 8192], P(('row', 'col')), may hold values from -6 to 6
- query_grads: bfloat16 [256, 8192], P(('row', 'col')), may hold values from -6 to 6
- input_basis: bfloat16 [8192, 8192], P('row', 'col'), may hold values from -0.0625 to 0.0625
- output_basis: bfloat16 [8192, 8192], P('col', 'row'), may hold values from -0.0625 to 0.0625
- eigenvalues: float32 [8192, 8192], P('row', 'col'), may hold values from 0.5 to 5
- query_starts: int32 [16], replicated, may hold values from 0 to 255, as said below
- query_ends: int32 [16], replicated, may hold values from 1 to 256, as said below
Outputs:
- scores: float32 [16, 512], replicated
Inputs may be any that keep to these rules, and one draw needn't show every extreme that they name: Query q covers the query rows query_starts[q] <= r < query_ends[q]: a nonempty span of at most 128 rows that lies inside one aligned block of 128 rows (rows k * 128 to (k + 1) * 128 - 1); spans of different queries may intersect or share a block. `query_ends`: see query_starts.
All inputs are finite; a program needn't handle non-finite values.
Results may differ from a plain program's by a relative error of at most 0.005.
Values may be sent and summed in bfloat16 or wider, within the bound.
A program may use at most 64 MiB of HBM per device.

v0:
```python
import math
import jax
import jax.numpy as jnp
from jax import lax
from jax.sharding import Mesh
from jax.sharding import PartitionSpec as P

D_IN = 8192
D_OUT = 8192
QBLOCK = 128
COL = ("col_0", "col_1", "col_2")
ROW = ("row_0", "row_1")
ROW_COL = ("row_0", "row_1", "col_0", "col_1", "col_2")
damping = 0.1


def laid_out(parts, dim):
    parts = jnp.moveaxis(parts, 0, dim)
    dims = parts.shape
    return parts.reshape(*dims[:dim], dims[dim] * dims[dim + 1], *dims[dim + 2 :])


def gather_together(arrays, axis, dims):
    line = jnp.concatenate([a.reshape(-1) for a in arrays])
    lines, at, gathered = (lax.all_gather(line, axis), 0, [])
    for a, dim in zip(arrays, dims):
        parts = lines[:, at : at + a.size].reshape(-1, *a.shape)
        gathered.append(laid_out(parts, dim))
        at += a.size
    return tuple(gathered)


def by_axis(value, axes):
    for axis in axes:
        value = lax.psum(value, axis)
    return value


def shards(
    train_inputs,
    train_grads,
    query_inputs,
    query_grads,
    input_basis,
    output_basis,
    eigenvalues,
    query_starts,
    query_ends,
):
    grouped = gather_together((train_inputs, query_inputs), COL, (0, 0))
    train_in, query_in = (
        lax.all_to_all(grouped[0], ROW, split_axis=1, concat_axis=0, tiled=True),
        lax.all_to_all(grouped[1], ROW, split_axis=1, concat_axis=0, tiled=True),
    )
    spread = (
        lax.all_to_all(train_grads, COL, split_axis=1, concat_axis=0, tiled=True),
        lax.all_to_all(query_grads, COL, split_axis=1, concat_axis=0, tiled=True),
    )
    train_out, query_out = gather_together((spread[0], spread[1]), ROW, (0, 0))
    train_in_part = jnp.dot(train_in, input_basis, preferred_element_type=jnp.float32)
    query_in_part = jnp.dot(query_in, input_basis, preferred_element_type=jnp.float32)
    train_out_part = jnp.dot(train_out, output_basis, preferred_element_type=jnp.float32)
    query_out_part = jnp.dot(query_out, output_basis, preferred_element_type=jnp.float32)
    in_sums = lax.psum((train_in_part, query_in_part), ROW)
    out_sums = lax.psum((train_out_part, query_out_part), COL)
    train_in_rot = in_sums[0].astype(jnp.bfloat16)
    query_in_rot = in_sums[1].astype(jnp.bfloat16)
    train_grad_rot = out_sums[0].astype(jnp.bfloat16)
    query_grad_rot = out_sums[1].astype(jnp.bfloat16)
    grads_wide = train_grad_rot.astype(jnp.float32)
    denominator = eigenvalues + damping

    def per_query(span):
        span_start, span_end = span
        block_top = span_start // QBLOCK * QBLOCK
        grad_rows = lax.dynamic_slice_in_dim(query_grad_rot, block_top, QBLOCK, 0)
        input_rows = lax.dynamic_slice_in_dim(query_in_rot, block_top, QBLOCK, 0)
        positions = block_top + jnp.arange(QBLOCK, dtype=jnp.int32)
        inside = (positions >= span_start) & (positions < span_end)
        grad_rows = jnp.where(inside[:, None], grad_rows, jnp.zeros((), grad_rows.dtype))
        outer_sum = lax.dot_general(
            grad_rows, input_rows, (((0,), (0,)), ((), ())), preferred_element_type=jnp.float32
        )
        scaled = (outer_sum / denominator).astype(jnp.bfloat16)
        paired = lax.dot_general(
            train_in_rot, scaled, (((1,), (1,)), ((), ())), preferred_element_type=jnp.float32
        )
        return jnp.sum(grads_wide * paired, axis=1)

    partial_scores = lax.map(per_query, (query_starts, query_ends))
    totals = by_axis(partial_scores, ROW_COL)
    return totals * (1.0 / math.sqrt(D_IN * D_OUT * QBLOCK))


def solution(mesh):
    split = Mesh(mesh.devices.reshape(4, 2, 2, 4, 2), ("row_0", "row_1", "col_0", "col_1", "col_2"))
    placed = (
        P(ROW_COL, None),
        P(ROW_COL, None),
        P(ROW_COL, None),
        P(ROW_COL, None),
        P(ROW, COL),
        P(COL, ROW),
        P(ROW, COL),
        P(),
        P(),
    )
    return jax.shard_map(shards, mesh=split, in_specs=placed, out_specs=P(), check_vma=False)
```

profile of v0, /device:TPU:1, one launch (start us, length us, event | category | flops | bytes accessed | tf_op | source)
XLA Modules:
  0.0 458.6 jit_solution(13673715249605043826)
XLA Ops:
  8.9 13.6 %all_to_all.70 = bf16[2,16,512]{2,0,1:T(2,128)(2,1)S(1)} all-to-all(bf16[2,16,512]{2,0,1:T(2,128)(2,1)} %bitcast.54), channel_id=1, replica_groups=mesh['row_0'=4,'row_1'=2,'col_0'=2,'col_1'=4,'col_2'=2] {'col_0','col_1'..., dimensions={1} | all-to-all | bytes 65536 | tf_op jit(solution)/shard_map/all_to_all | solution.py:57
  22.6 3.7 all-to-all-start
  26.2 3.2 broadcast_add_fusion
  32.2 31.4 %all-gather = bf16[393216]{0:T(1024)(128)(2,1)S(1)} all-gather(bf16[49152]{0:T(1024)(128)(2,1)S(1)} %pad_maximum_fusion), channel_id=2, replica_groups=mesh['row_0'=4,'row_1'=2,'col_0'=2,'col_1'=4,'col_2'=2] {'row_0','row_1'}, dimensions={0}, use_global_device_ids=true | all-gather | bytes 884736 | tf_op jit(solution)/shard_map/all_gather | solution.py:25
  70.1 4.5 all-to-all-start.2
  85.9 6.6 %all-to-all-start.3 = ((bf16[64,8,1024]{2,0,1:T(8,128)(2,1)}), bf16[64,8,1024]{2,0,1:T(8,128)(2,1)}, u32[]{:S(2)}, u32[]{:S(2)}) async-start(bf16[64,8,1024]{2,0,1:T(8,128)(2,1)} %copy.22), calls=%async_computation.3 | async-start | bytes 2097152 | tf_op jit(solution)/shard_map/all_to_all | solution.py:52
  92.6 74.4 %all-reduce.4 = (bf16[256,1024]{1,0:T(8,128)(2,1)}, bf16[512,1024]{1,0:T(8,128)(2,1)}) all-reduce(f32[256,1024]{1,0:T(8,128)} %fusion.15, f32[512,1024]{1,0:T(8,128)S(1)} %fusion.18), channel_id=1, replica_groups=mesh['row_0'=4,'row_1'=2,'col_0'=2,'col_1'=4,'col_2'=2] {'col_0','col_1'..., use_global_device_ids=true, to_apply=%region_0.0 | all-reduce | flops 786432 | bytes 4718592 | tf_op jit(solution)/shard_map/psum | solution.py:65
  171.0 3.3 fusion.17
  174.3 81.4 %all-reduce.5 = (bf16[256,512]{1,0:T(8,128)(2,1)}, bf16[512,512]{1,0:T(8,128)(2,1)}) all-reduce(f32[256,512]{1,0:T(8,128)} %fusion.16, f32[512,512]{1,0:T(8,128)} %fusion.17), channel_id=1, replica_groups=mesh['row_0'=4,'row_1'=2,'col_0'=2,'col_1'=4,'col_2'=2] {'row_0','row_1'}, use_global_device_ids=true, to_apply=%region_1.0 | all-reduce | flops 393216 | bytes 2359296 | tf_op jit(solution)/shard_map/psum | solution.py:64
  255.7 127.2 %while.12 = (s32[]{:T(128)}, f32[16,512]{1,0:T(8,128)S(1)}, s32[16]{0:T(128)S(1)}, s32[16]{0:T(128)S(1)}, bf16[256,1024]{1,0:T(8,128)(2,1)}, /*index=5*/bf16[256...) while((s32[]{:T(128)}, f32[16,512]{1,0:T(8,128)S(1)}, ...), condition=%wide.region_6.7_spmd, body=%wide.region_4.6_spmd.sunk | while | flops 673316864 | bytes 5119617 | solution.py:90
  260.6 2.9 fusion.35
  276.6 2.9 fusion.35
  284.5 2.9 fusion.35
  292.5 2.9 fusion.35
  308.4 2.9 fusion.35
  324.3 2.9 fusion.35
  340.2 2.9 fusion.35
  356.1 2.9 fusion.35
  372.0 2.9 fusion.35
  383.0 11.8 %psum.67 = f32[16,512]{1,0:T(8,128)S(1)} all-reduce(f32[16,512]{1,0:T(8,128)S(1)} %get-tuple-element.119), channel_id=1, replica_groups=mesh['row_0'=4,'row_1'=2,'col_0'=2,'col_1'=4,'col_2'=2] {'row_0'}, use_global_device_ids=true, to_apply=%region_7.8 | all-reduce | flops 8192 | bytes 65536 | tf_op jit(solution)/shard_map/psum | solution.py:35
  394.8 7.5 %psum.68 = f32[16,512]{1,0:T(8,128)S(1)} all-reduce(f32[16,512]{1,0:T(8,128)S(1)} %psum.67), channel_id=1, replica_groups=mesh['row_0'=4,'row_1'=2,'col_0'=2,'col_1'=4,'col_2'=2] {'row_1'}, use_global_device_ids=true, to_apply=%region_8.9 | all-reduce | flops 8192 | bytes 65536 | tf_op jit(solution)/shard_map/psum | solution.py:35
  402.3 6.6 %psum.69 = f32[16,512]{1,0:T(8,128)S(1)} all-reduce(f32[16,512]{1,0:T(8,128)S(1)} %psum.68), channel_id=1, replica_groups=mesh['row_0'=4,'row_1'=2,'col_0'=2,'col_1'=4,'col_2'=2] {'col_0'}, use_global_device_ids=true, to_apply=%region_9.10 | all-reduce | flops 8192 | bytes 65536 | tf_op jit(solution)/shard_map/psum | solution.py:35
  409.0 18.8 %psum.70 = f32[16,512]{1,0:T(8,128)S(1)} all-reduce(f32[16,512]{1,0:T(8,128)S(1)} %psum.69), channel_id=1, replica_groups=mesh['row_0'=4,'row_1'=2,'col_0'=2,'col_1'=4,'col_2'=2] {'col_1'}, use_global_device_ids=true, to_apply=%region_10.11 | all-reduce | flops 8192 | bytes 65536 | tf_op jit(solution)/shard_map/psum | solution.py:35
  427.7 23.4 %psum.71 = f32[16,512]{1,0:T(8,128)S(1)} all-reduce(f32[16,512]{1,0:T(8,128)S(1)} %psum.70), channel_id=1, replica_groups=mesh['row_0'=4,'row_1'=2,'col_0'=2,'col_1'=4,'col_2'=2] {'col_2'}, use_global_device_ids=true, to_apply=%region_11.12 | all-reduce | flops 8192 | bytes 65536 | tf_op jit(solution)/shard_map/psum | solution.py:35
  (114 shorter events, 88.1 us)
Async XLA Ops:
  6.5 68.1 %copy-start = (bf16[512,1024]{1,0:T(8,128)(2,1)S(1)}, bf16[512,1024]{1,0:T(8,128)(2,1)}, u32[]{:S(2)}) copy-start(bf16[512,1024]{1,0:T(8,128)(2,1)} %param.16) | copy-start | bytes 3145732
  6.5 58.5 %all-gather.4.cloned.1.call-start = ((), (), s32[]{:S(2)}) async-start(), calls=%async_computation.4 | async-start | bytes 1671168 | tf_op jit(solution)/shard_map/all_gather | solution.py:25
  22.6 9.6 %all-to-all-start = ((bf16[4,16,512]{2,0,1:T(4,128)(2,1)}), bf16[4,16,512]{2,0,1:T(4,128)(2,1)S(1)}, u32[]{:S(2)}, u32[]{:S(2)}) async-start(bf16[4,16,512]{2,0,1:T(4,128)(2,1)} %bitcast.51), calls=%async_computation | async-start | bytes 131072 | tf_op jit(solution)/shard_map/all_to_all | solution.py:56
  63.9 1.1 copy-start.3
  66.8 3.3 copy-start.1
  70.1 6.3 %slice-start = ((bf16[8,49152]{1,0:T(8,128)(2,1)}), bf16[8,16384]{1,0:T(8,128)(2,1)S(1)}, s32[]{:S(2)}) async-start(bf16[8,49152]{1,0:T(8,128)(2,1)} %copy-done.3), calls=%async_computation.5 | async-start | bytes 524288 | tf_op jit(solution)/shard_map/slice | solution.py:27
  70.1 15.8 %all-to-all-start.2 = ((bf16[32,8,1024]{2,0,1:T(8,128)(2,1)}), bf16[32,8,1024]{2,0,1:T(8,128)(2,1)}, u32[]{:S(2)}, u32[]{:S(2)}) async-start(bf16[32,8,1024]{2,0,1:T(8,128)(2,1)} %copy.21), calls=%async_computation.2 | async-start | bytes 1048576 | tf_op jit(solution)/shard_map/all_to_all | solution.py:53
  77.2 2.5 copy-start.2
  85.9 85.1 %all-to-all-start.3 = ((bf16[64,8,1024]{2,0,1:T(8,128)(2,1)}), bf16[64,8,1024]{2,0,1:T(8,128)(2,1)}, u32[]{:S(2)}, u32[]{:S(2)}) async-start(bf16[64,8,1024]{2,0,1:T(8,128)(2,1)} %copy.22), calls=%async_computation.3 | async-start | bytes 2097152 | tf_op jit(solution)/shard_map/all_to_all | solution.py:52
  171.0 84.7 %copy-start.4 = (s32[16]{0:T(128)S(1)}, s32[16]{0:T(128)}, u32[]{:S(2)}) copy-start(s32[16]{0:T(128)} %param.18) | copy-start | bytes 196
  171.0 84.7 %copy-start.5 = (s32[16]{0:T(128)S(1)}, s32[16]{0:T(128)}, u32[]{:S(2)}) copy-start(s32[16]{0:T(128)} %param.19) | copy-start | bytes 196
Sparse Core Ops, SparseCore 0:
  9.1 38.4 all-gather.3
where the time goes:
time: 461 us; the launch traced here: 459 us
  blocking collectives  269 us (58%)
  matrix products  56.8 us (12%)
  loops' own time  40.5 us (9%)
  local copies, waits for them, and re-layouts  37.2 us (8%)
  other arithmetic  24.1 us (5%)
  starting transfers between devices  14.8 us (3%)
  between operations  13.5 us (3%)
    psum x1, blocking collectives, shards(): in_sums = lax.psum((train_in_part, query_in_part), ROW)  81.4 us
    psum x1, blocking collectives, shards(): out_sums = lax.psum((train_out_part, query_out_part), COL)  74.4 us
    psum x5, blocking collectives, by_axis(): value = lax.psum(value, axis)  68.1 us
    dot_general x16, matrix products, per_query(): lax.dot_general(train_in_rot, scaled, (((1,), (1,)), ((), ())), preferred...  46.7 us
    another operation x1, loops' own time, shards(): partial_scores = lax.map(per_query, (query_starts, query_ends))  40.5 us
    all_gather x1, blocking collectives, gather_together(): lines, at, gathered = (lax.all_gather(line, axis), 0, [])  31.4 us
    and x16, other arithmetic, per_query(): inside = (positions >= span_start) & (positions < span_end)  19.6 us
    dynamic_slice x32, local copies, waits for them, and re-layouts, shards(): partial_scores = lax.map(per_query, (query_starts, query_ends))  19.4 us
  transfers between devices with their start and end apart: 4, of which 1 were waited for; matrix products, arithmetic and copies ran while one was open for 4% of the time, Pallas kernels for 0%

commit v1 on v0

--- a/solution.py
+++ b/solution.py
@@ -61,7 +61,8 @@
     query_in_part = jnp.dot(query_in, input_basis, preferred_element_type=jnp.float32)
     train_out_part = jnp.dot(train_out, output_basis, preferred_element_type=jnp.float32)
     query_out_part = jnp.dot(query_out, output_basis, preferred_element_type=jnp.float32)
-    in_sums = lax.psum((train_in_part, query_in_part), ROW)
+    pair_roots = lambda obj: lax.psum(lax.psum(obj, axis_name="row_1"), axis_name="row_0")
+    in_sums = pair_roots((train_in_part, query_in_part))
     out_sums = lax.psum((train_out_part, query_out_part), COL)
     train_in_rot = in_sums[0].astype(jnp.bfloat16)
     query_in_rot = in_sums[1].astype(jnp.bfloat16)

time: 461 us -> 444 us (0.963)
  blocking collectives: 269 us -> 235 us
  waiting for transfers between devices: 2.68 us -> 23.1 us
    psum x1, blocking collectives: 81.4 us -> 32.8 us  [shards(): lax.psum(lax.psum(obj, axis_name='row_1'), axis_name='row_0')]
    all_gather x1, waiting for transfers between devices: 0.01 us -> 19.8 us  [gather_together(): lines, at, gathered = (lax.all_gather(line, axis), 0, [])]
    psum x1, blocking collectives: 74.4 us -> 92.3 us  [shards(): out_sums = lax.psum((train_out_part, query_out_part), COL)]
    psum x5, blocking collectives: 68.1 us -> 56.5 us  [by_axis(): value = lax.psum(value, axis)]
    all_gather x1, blocking collectives: 31.4 us -> 39.5 us  [gather_together(): lines, at, gathered = (lax.all_gather(line, axis), 0, [])]
  transfers between devices with their start and end apart: 4 -> 5, of which waited for: 1 -> 2; matrix products, arithmetic and copies ran while one was open for 4% -> 5% of each run, Pallas kernels for 0% -> 0%
where the time goes in v1:
time: 444 us; the launch traced here: 442 us
  blocking collectives  235 us (53%)
  matrix products  56.6 us (13%)
  loops' own time  40.5 us (9%)
  local copies, waits for them, and re-layouts  35.1 us (8%)
  other arithmetic  24.1 us (5%)
  waiting for transfers between devices  23.1 us (5%)
  starting transfers between devices  14.1 us (3%)
  between operations  13.6 us (3%)
    psum x1, blocking collectives, shards(): out_sums = lax.psum((train_out_part, query_out_part), COL)  92.3 us
    psum x5, blocking collectives, by_axis(): value = lax.psum(value, axis)  56.5 us
    dot_general x16, matrix products, per_query(): lax.dot_general(train_in_rot, scaled, (((1,), (1,)), ((), ())), preferred...  46.7 us
    another operation x1, loops' own time, shards(): partial_scores = lax.map(per_query, (query_starts, query_ends))  40.5 us
    all_gather x1, blocking collectives, gather_together(): lines, at, gathered = (lax.all_gather(line, axis), 0, [])  39.5 us
    psum x1, blocking collectives, shards(): lax.psum(lax.psum(obj, axis_name='row_1'), axis_name='row_0')  32.8 us
    all_gather x1, waiting for transfers between devices, gather_together(): lines, at, gathered = (lax.all_gather(line, axis), 0, [])  19.8 us
    and x16, other arithmetic, per_query(): inside = (positions >= span_start) & (positions < span_end)  19.6 us
  transfers between devices with their start and end apart: 5, of which 2 were waited for; matrix products, arithmetic and copies ran while one was open for 5% of the time, Pallas kernels for 0%

profile of v1, /device:TPU:1, one launch (start us, length us, event | category | flops | bytes accessed | tf_op | source)
XLA Modules:
  0.0 441.8 jit_solution(4286991284614033062)
XLA Ops:
  8.9 13.6 %all_to_all.70 = bf16[2,16,512]{2,0,1:T(2,128)(2,1)S(1)} all-to-all(bf16[2,16,512]{2,0,1:T(2,128)(2,1)} %bitcast.55), channel_id=1, replica_groups=mesh['row_0'=4,'row_1'=2,'col_0'=2,'col_1'=4,'col_2'=2] {'col_0','col_1'..., dimensions={1} | all-to-all | bytes 65536 | tf_op jit(solution)/shard_map/all_to_all | solution.py:57
  22.6 3.7 all-to-all-start
  26.2 19.8 %all-gather.4.cloned.1.call-done = bf16[786432]{0:T(1024)(128)(2,1)} async-done(((bf16[49152]{0:T(1024)(128)(2,1)}), bf16[786432]{0:T(1024)(128)(2,1)}) %all-gather.4.cloned.1.call-update) | async-done | bytes 1572880 | tf_op jit(solution)/shard_map/all_gather | solution.py:25
  51.1 6.1 %all-to-all-start.2 = ((bf16[32,8,1024]{2,0,1:T(8,128)(2,1)}), bf16[32,8,1024]{2,0,1:T(8,128)(2,1)S(1)}, u32[]{:S(2)}, u32[]{:S(2)}) async-start(bf16[32,8,1024]{2,0,1:T(8,128)(2,1)} %copy.21), calls=%async_computation.2 | async-start | bytes 1048576 | tf_op jit(solution)/shard_map/all_to_all | solution.py:53
  57.2 3.2 broadcast_add_fusion
  64.6 3.3 all-to-all-done.2
  67.9 4.2 all-to-all-start.3
  72.2 39.5 %all-gather = bf16[393216]{0:T(1024)(128)(2,1)S(1)} all-gather(bf16[49152]{0:T(1024)(128)(2,1)S(1)} %pad_maximum_fusion), channel_id=2, replica_groups=mesh['row_0'=4,'row_1'=2,'col_0'=2,'col_1'=4,'col_2'=2] {'row_0','row_1'}, dimensions={0}, use_global_device_ids=true | all-gather | bytes 884736 | tf_op jit(solution)/shard_map/all_gather | solution.py:25
  115.6 3.2 fusion.17
  123.9 92.3 %all-reduce.9 = (bf16[256,1024]{1,0:T(8,128)(2,1)}, bf16[512,1024]{1,0:T(8,128)(2,1)}) all-reduce(f32[256,1024]{1,0:T(8,128)} %fusion.15, f32[512,1024]{1,0:T(8,128)S(1)} %fusion.18), channel_id=1, replica_groups=mesh['row_0'=4,'row_1'=2,'col_0'=2,'col_1'=4,'col_2'=2] {'col_0','col_1'..., use_global_device_ids=true, to_apply=%region_0.0 | all-reduce | flops 786432 | bytes 4718592 | tf_op jit(solution)/shard_map/psum | solution.py:66
  217.8 32.8 %all-reduce.8 = (bf16[256,512]{1,0:T(8,128)(2,1)}, bf16[512,512]{1,0:T(8,128)(2,1)}) all-reduce(f32[256,512]{1,0:T(8,128)} %get-tuple-element.178, f32[512,512]{1,0:T(8,128)} %get-tuple-element.179), channel_id=1, replica_groups=mesh['row_0'=4,'row_1'=2,'col_0'=2,'col_1'=4,'col_2'=2] {'row_0'}, use_global_device_ids=true, to_apply=%region_2.0 | all-reduce | flops 393216 | bytes 2359296 | tf_op jit(solution)/shard_map/psum | solution.py:64
  250.6 127.2 %while.12 = (s32[]{:T(128)}, f32[16,512]{1,0:T(8,128)S(1)}, s32[16]{0:T(128)S(1)}, s32[16]{0:T(128)S(1)}, bf16[256,1024]{1,0:T(8,128)(2,1)}, /*index=5*/bf16[256...) while((s32[]{:T(128)}, f32[16,512]{1,0:T(8,128)S(1)}, ...), condition=%wide.region_8.9_spmd, body=%wide.region_6.8_spmd.sunk | while | flops 673316864 | bytes 5119617 | solution.py:91
  271.4 2.9 fusion.35
  287.3 2.9 fusion.35
  303.2 2.9 fusion.35
  319.1 2.9 fusion.35
  335.0 2.9 fusion.35
  350.9 2.9 fusion.35
  366.9 2.9 fusion.35
  377.8 11.9 %psum.83 = f32[16,512]{1,0:T(8,128)S(1)} all-reduce(f32[16,512]{1,0:T(8,128)S(1)} %get-tuple-element.119), channel_id=1, replica_groups=mesh['row_0'=4,'row_1'=2,'col_0'=2,'col_1'=4,'col_2'=2] {'row_0'}, use_global_device_ids=true, to_apply=%region_9.10 | all-reduce | flops 8192 | bytes 65536 | tf_op jit(solution)/shard_map/psum | solution.py:35
  389.7 7.3 %psum.84 = f32[16,512]{1,0:T(8,128)S(1)} all-reduce(f32[16,512]{1,0:T(8,128)S(1)} %psum.83), channel_id=1, replica_groups=mesh['row_0'=4,'row_1'=2,'col_0'=2,'col_1'=4,'col_2'=2] {'row_1'}, use_global_device_ids=true, to_apply=%region_10.11 | all-reduce | flops 8192 | bytes 65536 | tf_op jit(solution)/shard_map/psum | solution.py:35
  397.0 6.5 %psum.85 = f32[16,512]{1,0:T(8,128)S(1)} all-reduce(f32[16,512]{1,0:T(8,128)S(1)} %psum.84), channel_id=1, replica_groups=mesh['row_0'=4,'row_1'=2,'col_0'=2,'col_1'=4,'col_2'=2] {'col_0'}, use_global_device_ids=true, to_apply=%region_11.12 | all-reduce | flops 8192 | bytes 65536 | tf_op jit(solution)/shard_map/psum | solution.py:35
  403.5 14.1 %psum.86 = f32[16,512]{1,0:T(8,128)S(1)} all-reduce(f32[16,512]{1,0:T(8,128)S(1)} %psum.85), channel_id=1, replica_groups=mesh['row_0'=4,'row_1'=2,'col_0'=2,'col_1'=4,'col_2'=2] {'col_1'}, use_global_device_ids=true, to_apply=%region_12.13 | all-reduce | flops 8192 | bytes 65536 | tf_op jit(solution)/shard_map/psum | solution.py:35
  417.6 16.8 %psum.87 = f32[16,512]{1,0:T(8,128)S(1)} all-reduce(f32[16,512]{1,0:T(8,128)S(1)} %psum.86), channel_id=1, replica_groups=mesh['row_0'=4,'row_1'=2,'col_0'=2,'col_1'=4,'col_2'=2] {'col_2'}, use_global_device_ids=true, to_apply=%region_13.14 | all-reduce | flops 8192 | bytes 65536 | tf_op jit(solution)/shard_map/psum | solution.py:35
  (113 shorter events, 89.0 us)
Async XLA Ops:
  6.5 112.3 %copy-start = (bf16[512,1024]{1,0:T(8,128)(2,1)S(1)}, bf16[512,1024]{1,0:T(8,128)(2,1)}, u32[]{:S(2)}) copy-start(bf16[512,1024]{1,0:T(8,128)(2,1)} %param.16) | copy-start | bytes 3145732
  6.5 39.5 %all-gather.4.cloned.1.call-start = ((), (), s32[]{:S(2)}) async-start(), calls=%async_computation.4 | async-start | bytes 1671168 | tf_op jit(solution)/shard_map/all_gather | solution.py:25
  22.6 28.5 %all-to-all-start = ((bf16[4,16,512]{2,0,1:T(4,128)(2,1)}), bf16[4,16,512]{2,0,1:T(4,128)(2,1)S(1)}, u32[]{:S(2)}, u32[]{:S(2)}) async-start(bf16[4,16,512]{2,0,1:T(4,128)(2,1)} %bitcast.52), calls=%async_computation | async-start | bytes 131072 | tf_op jit(solution)/shard_map/all_to_all | solution.py:56
  51.1 16.8 %all-to-all-start.2 = ((bf16[32,8,1024]{2,0,1:T(8,128)(2,1)}), bf16[32,8,1024]{2,0,1:T(8,128)(2,1)S(1)}, u32[]{:S(2)}, u32[]{:S(2)}) async-start(bf16[32,8,1024]{2,0,1:T(8,128)(2,1)} %copy.21), calls=%async_computation.2 | async-start | bytes 1048576 | tf_op jit(solution)/shard_map/all_to_all | solution.py:53
  67.9 47.7 %all-to-all-start.3 = ((bf16[64,8,1024]{2,0,1:T(8,128)(2,1)}), bf16[64,8,1024]{2,0,1:T(8,128)(2,1)}, u32[]{:S(2)}, u32[]{:S(2)}) async-start(bf16[64,8,1024]{2,0,1:T(8,128)(2,1)} %copy.22), calls=%async_computation.3 | async-start | bytes 2097152 | tf_op jit(solution)/shard_map/all_to_all | solution.py:52
  72.1 145.6 %all-reduce.7.cloned.1.call-start = ((), (), s32[]{:S(2)}) async-start(), calls=%async_computation.5 | async-start | bytes 3145728 | tf_op jit(solution)/shard_map/psum | solution.py:64
  112.1 3.5 copy-start.1
  118.9 1.8 slice-start
  216.2 34.4 %copy-start.2 = (s32[16]{0:T(128)S(1)}, s32[16]{0:T(128)}, u32[]{:S(2)}) copy-start(s32[16]{0:T(128)} %param.18) | copy-start | bytes 196
  216.2 34.4 %copy-start.3 = (s32[16]{0:T(128)S(1)}, s32[16]{0:T(128)}, u32[]{:S(2)}) copy-start(s32[16]{0:T(128)} %param.19) | copy-start | bytes 196
Sparse Core Ops, SparseCore 0:
  9.1 36.9 all-gather.3
  119.0 74.7 all-reduce.6
